TPU v7x, 32 devices: a whole 2x2x4 slice. The times are simulated.
32 devices in a mesh: section: 2 (over x), azim: 4 (over z), axial: 4 (over y, core).
Axes of the slice: x: 2, y: 2, z: 4, core: 2. Of those that a mesh axis runs over, the one named last changes fastest.
Arguments:
- magnetic_vector_field: float32 [3, 4, 512, 512], P(None, 'azim', 'section', 'axial'), may hold values from -3 to 3
- imposed_current_density: float32 [3, 4, 512, 512], P(None, 'azim', 'section', 'axial'), may hold values from -6 to 6
- fixed_material_map: int32 [4, 512, 512], P('azim', 'section', 'axial'), may hold values from 0 to 7
- spinning_material_map: int32 [4, 128], replicated, may hold values from 0 to 7
- slab_slide_offsets: int32 [512], P('axial'), may hold values from 0 to 3, as said below
- inverse_permeability: float32 [8], replicated, may hold values from 0.1 to 1
- electric_conductance: float32 [8], replicated, may hold values from 0.05 to 0.5
- core_dissipation_coefficient: float32 [8], replicated, may hold values from 0.2 to 2
- inplane_thermal_conductance: float32 [8], replicated, may hold values from 1 to 4
- through_plane_conductance: float32 [8], replicated, may hold values from 0.1 to 0.5
- thermal_storage: float32 [8], replicated, may hold values from 0.05 to 0.3
- prior_thermal_state: float32 [4, 512, 512], P(None, ('section', 'azim'), 'axial'), may hold values from -6 to 6
- goal_sensitivity: float32 [4, 512, 512], P(None, ('section', 'azim'), 'axial'), may hold values from -16 to 16
Outputs:
- magnetic_misfit: float32 [3, 4, 512, 512], P(None, 'azim', 'section', 'axial')
- dual_magnetic_rhs: float32 [3, 4, 512, 512], P(None, 'azim', 'section', 'axial')
- thermal_state: float32 [4, 512, 512], P('azim', 'section', 'axial')
Inputs may be any that keep to these rules, and one draw needn't show every extreme that they name: `slab_slide_offsets`: the smallest and the largest offset each occur at some layer.
All inputs are finite; a program needn't handle non-finite values.
Results may differ from a plain program's by a relative error of at most 0.00002.
Values sent between devices are 32-bit elements; how exact they have to be, the bound alone decides.
A program may use at most 64 MiB of HBM per device.

v0:
```python
import functools

import jax
import jax.numpy as jnp
from jax import lax
from jax.experimental import pallas as pl
from jax.experimental.pallas import tpu as pltpu
from jax.sharding import PartitionSpec as P

SWEEPS = 4
RIM = 8
MESH = pl.DeviceIdType.MESH


def pick(bits, table):
    low, mid, high = bits
    pairs = [jnp.where(low, table[2 * i + 1], table[2 * i]) for i in range(4)]
    return jnp.where(high, jnp.where(mid, pairs[3], pairs[2]), jnp.where(mid, pairs[1], pairs[0]))


def bits_of(regions):
    return ((regions & 1) != 0, (regions & 2) != 0, (regions & 4) != 0)


def kernel(sizes, *refs):
    S, N, C = sizes
    (A_hbm, J_hbm, fixed, spin, offs, t_rel, t_eddy, t_loss, t_plane, t_axial, t_cap, prior, goal,
     misfit, dual, temp,
     AN, AX, AR, HN, HX, HR, regE, lossM, srcE, flux, H,
     priorX, goalX, regX, srcX,
     wa, wr, wl, inv, capH, rhsT, vT, vA, finT, finA, retA,
     A, J, relayG, relayP, local, send, recv) = refs
    R, L = fixed.shape
    rows = prior.shape[1]
    RROT = spin.shape[1]
    ext = rows + 2 * RIM
    s, j, c = lax.axis_index("section"), lax.axis_index("azim"), lax.axis_index("axial")
    Q = S * N
    q = s * N + j

    def section_id(d):
        return (lax.rem(s + d + S, S), j, c)

    def axial_id(d):
        return (s, j, lax.rem(c + d + C, C))

    def azim_id(d):
        return (s, lax.rem(j + d + N, N), c)

    barrier = pltpu.get_barrier_semaphore()
    partners = [azim_id(d) for d in range(1, N)]
    partners += [near(d) for near in (section_id, axial_id) for d in (1, -1)]
    for partner in partners:
        pl.semaphore_signal(barrier, inc=1, device_id=partner, device_id_type=MESH)

    loads = [
        pltpu.make_async_copy(A_hbm, A, local.at[0]),
        pltpu.make_async_copy(goal, goalX.at[1, :, pl.ds(RIM, rows), :], local.at[1]),
        pltpu.make_async_copy(prior, priorX.at[1, :, pl.ds(RIM, rows), :], local.at[2]),
        pltpu.make_async_copy(J_hbm, J, local.at[3]),
    ]
    for load in loads:
        load.start()

    counter = [0]
    pending = []

    def copy(src, dst, device, sending=None, receiving=None, later=False):
        k = counter[0]
        counter[0] += 1
        desc = pltpu.make_async_remote_copy(
            src_ref=src, dst_ref=dst, send_sem=send.at[k], recv_sem=recv.at[k],
            device_id=device, device_id_type=MESH)
        if later:
            pass
        elif sending is None:
            desc.start()
        else:
            pl.when(sending)(lambda: desc.start())
        pending.append((desc, sending))

        def arrive():
            if receiving is None:
                desc.wait_recv()
            else:
                pl.when(receiving)(lambda: desc.wait_recv())
        return (desc, arrive) if later else arrive

    def both(*conds):
        return functools.reduce(jnp.logical_and, conds)

    top, bottom = j == 0, j == N - 1
    before, after = s > 0, s < S - 1

    def forward(X):
        return [copy(X.at[1], X.at[2], axial_id(-1), c > 0, c < C - 1),
                copy(X.at[1], X.at[0], axial_id(1), c < C - 1, c > 0)]

    def centre(src, X):
        part = pl.ds(RIM, rows)
        return [copy(src, X.at[2, :, part, :], axial_id(-1), c > 0, c < C - 1),
                copy(src, X.at[0, :, part, :], axial_id(1), c < C - 1, c > 0)]

    def outer(X):
        arrivals = []
        for part in (pl.ds(0, RIM), pl.ds(RIM + rows, RIM)):
            own = X.at[1, :, part, :]
            arrivals.append(copy(own, X.at[2, :, part, :], axial_id(-1), c > 0, c < C - 1))
            arrivals.append(copy(own, X.at[0, :, part, :], axial_id(1), c < C - 1, c > 0))
        return arrivals

    def rims(src, X, relay):
        low, high = X.at[1, :, pl.ds(0, RIM), :], X.at[1, :, pl.ds(RIM + rows, RIM), :]
        first, last = src.at[:, 0:RIM, :], src.at[:, rows - RIM:rows, :]
        arrivals = [
            copy(last, low, azim_id(1), jnp.logical_not(bottom), jnp.logical_not(top)),
            copy(first, high, azim_id(-1), jnp.logical_not(top), jnp.logical_not(bottom))]
        crossed = [
            copy(last, relay.at[0], section_id(1), both(bottom, after), both(bottom, before)),
            copy(first, relay.at[1], section_id(-1), both(top, before), both(top, after))]

        def relayed():
            for arrive in crossed:
                arrive()
            arrivals.append(copy(relay.at[0], low, azim_id(1), both(bottom, before), both(top, before)))
            arrivals.append(copy(relay.at[1], high, azim_id(-1), both(top, after), both(bottom, after)))
            return arrivals
        return relayed

    def spread(E, target):
        edges = [copy(E.at[R:R + RIM, :], E.at[0:RIM, :], section_id(1), after, before),
                 copy(E.at[RIM:2 * RIM, :], E.at[R + RIM:R + 2 * RIM, :], section_id(-1), before, after)]
        arrivals, waiting = [], []
        for d in range(1, N):
            peer = lax.rem(j + d, N)
            desc, arrive = copy(
                E.at[pl.ds(pl.multiple_of(peer * rows, 8), ext), :], target.at[1, j], azim_id(d),
                later=True)
            needs = jnp.logical_or(both(peer == 0, before), both(peer == N - 1, after))
            pl.when(jnp.logical_not(needs))(lambda: desc.start())
            arrivals.append(arrive)
            waiting.append((desc, needs))

        def rest():
            for arrive in edges:
                arrive()
            for desc, needs in waiting:
                pl.when(needs)(lambda: desc.start())
            target[1, j] = E[pl.ds(pl.multiple_of(j * rows, 8), ext), :]
            return arrivals
        return rest

    lane = lax.broadcasted_iota(jnp.int32, (R, L), 1)
    row = lax.broadcasted_iota(jnp.int32, (R, L), 0)
    shift = j - offs[...]
    shift = jnp.broadcast_to(jnp.where(shift < 0, shift + N, shift), (RROT, L))
    rotor = jnp.zeros((RROT, L), jnp.float32)
    for m in range(N):
        column = jnp.transpose(jnp.broadcast_to(spin[m:m + 1, :].astype(jnp.float32), (L, RROT)))
        rotor = jnp.where(shift == m, column, rotor)
    regE[RIM:RIM + R, :] = fixed[...]
    regE[RIM:RIM + RROT, :] = jnp.where(s == 0, rotor.astype(jnp.int32), fixed[0:RROT, :])

    lossM[...] = pick(bits_of(regE[RIM:RIM + R, :]), t_loss)
    pl.semaphore_wait(barrier, len(partners))

    got_an = copy(A_hbm.at[1:3], AN, azim_id(-1))
    got_ax = copy(A_hbm.at[0:2], AX, axial_id(-1), c > 0, c < C - 1)
    got_ar = copy(A_hbm.at[:, 0:RIM, :], AR, section_id(-1), before, after)

    rest_reg = spread(regE, regX)
    rest_goal = rims(goal, goalX, relayG)
    rest_prior = rims(prior, priorX, relayP)
    goal_centre, prior_centre = centre(goal, goalX), centre(prior, priorX)
    got_reg = rest_reg()
    got_goal, got_prior = rest_goal(), rest_prior()

    loads[0].wait()

    got_ax()
    got_ar()
    last_lane, last_row = c == C - 1, s == S - 1

    def lane_up(values, beside):
        beside = jnp.where(last_lane, 0.0, beside)
        return pltpu.roll(jnp.where(lane == 0, beside, values), L - 1, 1)

    def row_up(values, beside):
        beside = jnp.where(last_row, 0.0, beside)
        return jnp.where(row == R - 1, beside, pltpu.roll(values, R - 1, 0))

    flux[0] = (row_up(A[2], AR[2, 0:1, :]) - A[2]) - (lane_up(A[1], AX[1]) - A[1])
    flux[1] = lane_up(A[0], AX[0]) - A[0]
    flux[2] = A[0] - row_up(A[0], AR[0, 0:1, :])
    got_an()
    f0 = flux[0]
    f1 = flux[1] - (AN[1] - A[2])
    f2 = flux[2] + (AN[0] - A[1])
    flux[1] = f1
    flux[2] = f2
    srcE[RIM:RIM + R, :] = lossM[...] * (f0 * f0 + f1 * f1 + f2 * f2)
    rest_src = spread(srcE, srcX)
    for arrive in got_reg:
        arrive()
    got_reg = forward(regX)
    reluct = pick(bits_of(regE[RIM:RIM + R, :]), t_rel)
    H[0] = reluct * flux[0]
    H[1] = reluct * flux[1]
    H[2] = reluct * flux[2]
    got_src = rest_src()
    got_hn = copy(H.at[1:3], HN, azim_id(1))
    got_hr = copy(H.at[:, R - RIM:R, :], HR, section_id(1), after, before)

    for load, arrivals in ((loads[1], got_goal), (loads[2], got_prior)):
        load.wait()
        for arrive in arrivals:
            arrive()
    got_goal = goal_centre + outer(goalX)
    got_prior = prior_centre + outer(priorX)

    def ext_mask():
        grow = lax.broadcasted_iota(jnp.int32, (ext, 2 * L), 0) + (q * rows - RIM)
        glane = lax.broadcasted_iota(jnp.int32, (ext, 2 * L), 1)
        ok = jnp.logical_and(grow >= 0, grow < Q * rows)
        right = jnp.logical_and(glane >= L, glane < L + L // 2)
        left = glane >= L + L // 2
        ok = jnp.logical_and(ok, jnp.logical_not(jnp.logical_and(right, c == C - 1)))
        return jnp.logical_and(ok, jnp.logical_not(jnp.logical_and(left, c == 0)))

    half = lax.broadcasted_iota(jnp.int32, (ext, L), 1) < L // 2

    def wide(X, a):
        return jnp.concatenate([X[1, a], jnp.where(half, X[2, a], X[0, a])], axis=1)

    up = lambda x, axis: pltpu.roll(x, x.shape[axis] - 1, axis)
    down = lambda x, axis: pltpu.roll(x, 1, axis)

    def each(f):
        if N <= 8:
            for a in range(N):
                f(a, (a + 1) % N, (a + N - 1) % N)
        else:
            def step(a, carry):
                f(a, lax.rem(a + 1, N), lax.rem(a + N - 1, N))
                return carry
            lax.fori_loop(0, N, step, 0)

    for arrive in got_reg:
        arrive()

    def first(a, ap, am):
        bits = bits_of(wide(regX, a))
        ok = ext_mask()
        plane = jnp.where(ok, pick(bits, t_plane), 0.0)
        axial = jnp.where(ok, pick(bits, t_axial), 0.0)
        capH[a] = pick(bits, t_cap)
        inv[a] = plane
        wr[a] = 0.5 * (plane + up(plane, 0))
        wl[a] = 0.5 * (axial + up(axial, 1))

    def second(a, ap, am):
        wa[a] = 0.5 * (inv[a] + inv[ap])

    def third(a, ap, am):
        total = (wa[a] + wa[am]) + (wr[a] + down(wr[a], 0)) + (wl[a] + down(wl[a], 1)) + capH[a]
        inv[a] = jnp.where(ext_mask(), 1.0 / total, 0.0)

    each(first)
    each(second)
    each(third)

    for arrive in got_src:
        arrive()
    got_src = forward(srcX)
    got_hx = copy(H.at[0:2], HX, axial_id(1), c < C - 1, c > 0)

    def inflow(v, a, ap, am):
        x = v[a]
        r, l = wr[a], wl[a]
        return ((wa[a] * v[ap] + wa[am] * v[am]) + (r * up(x, 0) + down(r * x, 0))
                + (l * up(x, 1) + down(l * x, 1)))

    for arrive in got_goal:
        arrive()

    def adjoint_first(a, ap, am):
        rhs = jnp.where(ext_mask(), wide(goalX, a), 0.0)
        rhsT[a] = rhs
        vA[0, a] = rhs * inv[a]

    each(adjoint_first)

    def sweeps(v, count, final):
        for k in range(count):
            now, later = k % 2, (k + 1) % 2

            def one(a, ap, am):
                new = (rhsT[a] + inflow(v.at[now], a, ap, am)) * inv[a]
                if k == count - 1:
                    final[a] = new[RIM:RIM + rows, 0:L]
                else:
                    v[later, a] = new
            each(one)

    def gather(final, ret):
        arrivals = []
        for d in range(1, N):
            peer = lax.rem(j + d, N)
            arrivals.append(copy(
                final.at[peer], ret.at[pl.ds(pl.multiple_of(j * rows, 8), rows), :], azim_id(d)))
        ret[pl.ds(pl.multiple_of(j * rows, 8), rows), :] = final[j]
        return arrivals

    sweeps(vA, SWEEPS - 1, finA)
    got_adj = gather(finA, retA)

    for arrive in got_prior:
        arrive()
    for arrive in got_src:
        arrive()

    def thermal_first(a, ap, am):
        ok = ext_mask()
        start = jnp.where(ok, wide(priorX, a), 0.0)
        vT[0, a] = start
        rhsT[a] = capH[a] * start + jnp.where(ok, wide(srcX, a), 0.0)

    each(thermal_first)
    sweeps(vT, SWEEPS, finT)
    got_temp = gather(finT, temp)

    loads[3].wait()
    got_hn()
    got_hx()
    got_hr()

    def lane_down(values, beside):
        beside = jnp.where(c == 0, 0.0, beside)
        return pltpu.roll(jnp.where(lane == L - 1, beside, values), 1, 1)

    def row_down(values, beside):
        beside = jnp.where(s == 0, 0.0, beside)
        return jnp.where(row == 0, beside, pltpu.roll(values, 1, 0))

    eddy = pick(bits_of(regE[RIM:RIM + R, :]), t_eddy)
    h0, h1, h2 = H[0], H[1], H[2]
    rim0, rim2 = HR[0, RIM - 1:RIM, :], HR[2, RIM - 1:RIM, :]
    misfit[0] = (lane_down(h1, HX[1]) - h1) - (row_down(h2, rim2) - h2) + eddy * A[0] - J[0]
    misfit[1] = (HN[1] - h2) - (lane_down(h0, HX[0]) - h0) + eddy * A[1] - J[1]
    misfit[2] = (row_down(h0, rim0) - h0) - (HN[0] - h1) + eddy * A[2] - J[2]

    for arrive in got_adj:
        arrive()
    scale = 2.0 * lossM[...] * retA[...]
    for k in range(3):
        dual[k] = scale * flux[k]
    for arrive in got_temp:
        arrive()
    for desc, sending in pending:
        if sending is None:
            desc.wait_send()
        else:
            pl.when(sending)(lambda: desc.wait_send())


def store(*refs):
    sems = refs[6]
    copies = [pltpu.make_async_copy(refs[k], refs[3 + k], sems.at[k]) for k in range(3)]
    for one in copies:
        one.start()
    for one in copies:
        one.wait()


def body(sizes, *args):
    (A, J, fixed, spin, offs, rel, eddy, loss, plane, axial, cap, prior, goal) = args
    _, one, R, L = A.shape
    assert one == 1 and spin.shape[1] <= R
    S, N, C = sizes
    rows = prior.shape[1]
    ext = rows + 2 * RIM
    f32 = jnp.float32
    vmem = pl.BlockSpec(memory_space=pltpu.VMEM)
    hbm = pl.BlockSpec(memory_space=pl.ANY)
    smem = pl.BlockSpec(memory_space=pltpu.SMEM)
    V = lambda *shape, dtype=f32: pltpu.VMEM(shape, dtype)
    copies = 38 + 4 * (N - 1)
    wide = (N, ext, 2 * L)
    misfit, dual, temp = pl.pallas_call(
        functools.partial(kernel, sizes),
        out_shape=(V(3, R, L), V(3, R, L), V(R, L)),
        in_specs=[hbm] * 2 + [vmem] * 3 + [smem] * 6 + [hbm] * 2,
        out_specs=(vmem, vmem, vmem),
        scratch_shapes=[
            V(2, R, L), V(2, R, L), V(3, RIM, L), V(2, R, L), V(2, R, L), V(3, RIM, L),
            V(R + 2 * RIM, L, dtype=jnp.int32), V(R, L), V(R + 2 * RIM, L), V(3, R, L), V(3, R, L),
            V(3, N, ext, L), V(3, N, ext, L), V(3, N, ext, L, dtype=jnp.int32), V(3, N, ext, L),
            V(*wide), V(*wide), V(*wide), V(*wide), V(*wide), V(*wide), V(2, *wide), V(2, *wide),
            V(N, rows, L), V(N, rows, L), V(R, L), V(3, R, L), V(3, R, L),
            V(2, N, RIM, L), V(2, N, RIM, L), pltpu.SemaphoreType.DMA((4,)),
            pltpu.SemaphoreType.DMA((copies,)), pltpu.SemaphoreType.DMA((copies,)),
        ],
        compiler_params=pltpu.CompilerParams(collective_id=0, has_side_effects=True),
    )(A.reshape(3, R, L), J.reshape(3, R, L), fixed.reshape(R, L), spin, offs.reshape(1, L),
      rel, eddy, loss, plane, axial, cap, prior, goal)
    misfit, dual, temp = pl.pallas_call(
        store,
        out_shape=tuple(jax.ShapeDtypeStruct(x.shape, f32) for x in (misfit, dual, temp)),
        in_specs=[vmem] * 3,
        out_specs=(hbm, hbm, hbm),
        scratch_shapes=[pltpu.SemaphoreType.DMA((3,))],
    )(*(pltpu.with_memory_space_constraint(x, pltpu.VMEM) for x in (misfit, dual, temp)))
    return misfit.reshape(3, 1, R, L), dual.reshape(3, 1, R, L), temp.reshape(1, R, L)


def solution(mesh):
    sizes = (mesh.shape["section"], mesh.shape["azim"], mesh.shape["axial"])
    in_specs = (
        P(None, "azim", "section", "axial"),
        P(None, "azim", "section", "axial"),
        P("azim", "section", "axial"),
        P(),
        P("axial"),
        P(),
        P(),
        P(),
        P(),
        P(),
        P(),
        P(None, ("section", "azim"), "axial"),
        P(None, ("section", "azim"), "axial"),
    )
    out_specs = (
        P(None, "azim", "section", "axial"),
        P(None, "azim", "section", "axial"),
        P("azim", "section", "axial"),
    )
    return jax.shard_map(functools.partial(body, sizes), mesh=mesh, in_specs=in_specs,
                         out_specs=out_specs, check_vma=False)
```

profile of v0, /device:TPU:30, one launch (start us, length us, event | category | flops | bytes accessed | tf_op | source)
XLA Modules:
  0.0 41.8 jit_solution(1486219155553508787)
XLA Ops:
  0.6 40.2 %shard_map.148 = (f32[3,256,128]{2,1,0:T(8,128)S(1)}, f32[3,256,128]{2,1,0:T(8,128)S(1)}, f32[256,128]{1,0:T(8,128)S(1)}) custom-call(f32[3,256,128]{2,1,0:T(8,128)} %bitcast.11, f32[3,256,128]{2,1,0:T(8,128)} %bitcast.12, s32[256,128]{1,0:T(8,128)} %bitcast.13, s32[4,128]{1,0:T(4,128)} %refs_3_.1, s32[1,128]{1,0:T(1,128)} %bitcast.14, f32[8]{0:T(128)} %refs_5_.1, ...), custom_call_target="tpu_custom_call" | custom-call | tf_op jit(solution)/shard_map/pallas_call | solution.py:389
  40.9 0.9 %shard_map.149 = (f32[3,256,128]{2,1,0:T(8,128)}, f32[3,256,128]{2,1,0:T(8,128)}, f32[256,128]{1,0:T(8,128)}) custom-call(f32[3,256,128]{2,1,0:T(8,128)S(1)} %get-tuple-element.9.refs_0_, f32[3,256,128]{2,1,0:T(8,128)S(1)} %get-tuple-element.10.refs_1_, f32[256,128]{1,0:T(8,128)S(1)} %get-tuple-element.11.refs_2_), custom_call_target="tpu_custom_call" | custom-call | tf_op jit(solution)/shard_map/pallas_call | solution.py:406
where the time goes:
time: 42 us; the launch traced here: 41.8 us
  Pallas kernels  41.2 us (98%)
  between operations  0.64 us (2%)
    pallas_call x1, Pallas kernels, body(): pl.pallas_call(functools.partial(kernel, sizes), out_shape=(V(3, R, L), V...  40.2 us
    pallas_call x1, Pallas kernels, body(): pl.pallas_call(store, out_shape=tuple((jax.ShapeDtypeStruct(x.shape, f32)...  0.94 us

commit v1 on v0

--- a/solution.py
+++ b/solution.py
@@ -64,27 +64,32 @@
 
     counter = [0]
     pending = []
-
-    def copy(src, dst, device, sending=None, receiving=None, later=False):
+    finals = []
+
+    def slots(count):
         k = counter[0]
-        counter[0] += 1
-        desc = pltpu.make_async_remote_copy(
+        counter[0] += count
+        return k
+
+    def remote(src, dst, device, k):
+        return pltpu.make_async_remote_copy(
             src_ref=src, dst_ref=dst, send_sem=send.at[k], recv_sem=recv.at[k],
             device_id=device, device_id_type=MESH)
-        if later:
-            pass
-        elif sending is None:
-            desc.start()
+
+    def when(cond, f):
+        if cond is None:
+            f()
         else:
-            pl.when(sending)(lambda: desc.start())
+            pl.when(cond)(f)
+
+    def copy(src, dst, device, sending=None, receiving=None):
+        desc = remote(src, dst, device, slots(1))
+        when(sending, lambda: desc.start())
         pending.append((desc, sending))
-
-        def arrive():
-            if receiving is None:
-                desc.wait_recv()
-            else:
-                pl.when(receiving)(lambda: desc.wait_recv())
-        return (desc, arrive) if later else arrive
+        return lambda: when(receiving, lambda: desc.wait_recv())
+
+    def farthest(i):
+        return jnp.where(j < N // 2, N - i, i)
 
     def both(*conds):
         return functools.reduce(jnp.logical_and, conds)
@@ -128,27 +133,64 @@
         return relayed
 
     def spread(E, target):
+        inner = ext - RIM
+
+        def block(peer, slot, low, high, owner=j):
+            first, count = (RIM if low else 0), (inner if low or high else ext)
+            return remote(
+                E.at[pl.ds(pl.multiple_of(peer * rows + first, 8), count), :],
+                target.at[1, owner, pl.ds(first, count), :], (s, peer, c), slot)
+
+        def cases(peer, f):
+            pl.when(peer == 0)(lambda: f(True, False))
+            pl.when(peer == N - 1)(lambda: f(False, True))
+            pl.when(both(peer > 0, peer < N - 1))(lambda: f(False, False))
+
+        k = slots(N - 1)
+        for i in range(1, N):
+            d = farthest(i)
+            peer = lax.rem(j + d, N)
+            cases(peer, lambda low, high: block(peer, k + d - 1, low, high).start())
+        for d in range(1, N):
+            peer = lax.rem(j + d, N)
+            finals.append(lambda peer=peer, d=d: cases(
+                peer, lambda low, high: block(peer, k + d - 1, low, high).wait_send()))
         edges = [copy(E.at[R:R + RIM, :], E.at[0:RIM, :], section_id(1), after, before),
                  copy(E.at[RIM:2 * RIM, :], E.at[R + RIM:R + 2 * RIM, :], section_id(-1), before, after)]
-        arrivals, waiting = [], []
-        for d in range(1, N):
-            peer = lax.rem(j + d, N)
-            desc, arrive = copy(
-                E.at[pl.ds(pl.multiple_of(peer * rows, 8), ext), :], target.at[1, j], azim_id(d),
-                later=True)
-            needs = jnp.logical_or(both(peer == 0, before), both(peer == N - 1, after))
-            pl.when(jnp.logical_not(needs))(lambda: desc.start())
-            arrivals.append(arrive)
-            waiting.append((desc, needs))
 
         def rest():
             for arrive in edges:
                 arrive()
-            for desc, needs in waiting:
-                pl.when(needs)(lambda: desc.start())
+            ends = []
+            for peer, start, there in ((0, 0, before), (N - 1, RIM + rows, after)):
+                b = slots(N - 1)
+                d = lax.rem(peer - j + N, N)
+                own = E.at[start if peer == 0 else R + RIM:(start if peer == 0 else R + RIM) + RIM, :]
+                away = both(there, j != peer)
+                desc = remote(own, target.at[1, j, pl.ds(start, RIM), :], (s, peer, c),
+                              b + jnp.where(d > 0, d - 1, 0))
+                pl.when(away)(lambda desc=desc: desc.start())
+                pending.append((desc, away))
+                for d in range(1, N):
+                    got = remote(own, target.at[1, lax.rem(j - d + N, N), pl.ds(start, RIM), :],
+                                 (s, peer, c), b + d - 1)
+                    ends.append((got, both(there, j == peer)))
             target[1, j] = E[pl.ds(pl.multiple_of(j * rows, 8), ext), :]
-            return arrivals
+
+            def arrived():
+                for d in range(1, N):
+                    owner = lax.rem(j - d + N, N)
+                    cases(j, lambda low, high: block(j, k + d - 1, low, high, owner).wait_recv())
+                for got, here in ends:
+                    pl.when(here)(lambda got=got: got.wait_recv())
+            return arrived
         return rest
+
+    pl.semaphore_wait(barrier, len(partners))
+
+    got_an = copy(A_hbm.at[1:3], AN, azim_id(-1))
+    got_ax = copy(A_hbm.at[0:2], AX, axial_id(-1), c > 0, c < C - 1)
+    got_ar = copy(A_hbm.at[:, 0:RIM, :], AR, section_id(-1), before, after)
 
     lane = lax.broadcasted_iota(jnp.int32, (R, L), 1)
     row = lax.broadcasted_iota(jnp.int32, (R, L), 0)
@@ -161,17 +203,11 @@
     regE[RIM:RIM + R, :] = fixed[...]
     regE[RIM:RIM + RROT, :] = jnp.where(s == 0, rotor.astype(jnp.int32), fixed[0:RROT, :])
 
-    lossM[...] = pick(bits_of(regE[RIM:RIM + R, :]), t_loss)
-    pl.semaphore_wait(barrier, len(partners))
-
-    got_an = copy(A_hbm.at[1:3], AN, azim_id(-1))
-    got_ax = copy(A_hbm.at[0:2], AX, axial_id(-1), c > 0, c < C - 1)
-    got_ar = copy(A_hbm.at[:, 0:RIM, :], AR, section_id(-1), before, after)
-
     rest_reg = spread(regE, regX)
     rest_goal = rims(goal, goalX, relayG)
     rest_prior = rims(prior, priorX, relayP)
     goal_centre, prior_centre = centre(goal, goalX), centre(prior, priorX)
+    lossM[...] = pick(bits_of(regE[RIM:RIM + R, :]), t_loss)
     got_reg = rest_reg()
     got_goal, got_prior = rest_goal(), rest_prior()
 
@@ -200,23 +236,27 @@
     flux[2] = f2
     srcE[RIM:RIM + R, :] = lossM[...] * (f0 * f0 + f1 * f1 + f2 * f2)
     rest_src = spread(srcE, srcX)
-    for arrive in got_reg:
-        arrive()
-    got_reg = forward(regX)
     reluct = pick(bits_of(regE[RIM:RIM + R, :]), t_rel)
     H[0] = reluct * flux[0]
     H[1] = reluct * flux[1]
     H[2] = reluct * flux[2]
+    got_hr = copy(H.at[:, R - RIM:R, :], HR, section_id(1), after, before)
     got_src = rest_src()
-    got_hn = copy(H.at[1:3], HN, azim_id(1))
-    got_hr = copy(H.at[:, R - RIM:R, :], HR, section_id(1), after, before)
-
+
+    got_reg()
+    got_reg = forward(regX)
     for load, arrivals in ((loads[1], got_goal), (loads[2], got_prior)):
         load.wait()
         for arrive in arrivals:
             arrive()
     got_goal = goal_centre + outer(goalX)
     got_prior = prior_centre + outer(priorX)
+
+    got_src()
+    got_src = forward(srcX)
+    ring = remote(H.at[1:3], HN, azim_id(1), slots(1))
+    pl.when(j < N - 1)(lambda: ring.start())
+    got_hx = copy(H.at[0:2], HX, axial_id(1), c < C - 1, c > 0)
 
     def ext_mask():
         grow = lax.broadcasted_iota(jnp.int32, (ext, 2 * L), 0) + (q * rows - RIM)
@@ -269,11 +309,6 @@
     each(second)
     each(third)
 
-    for arrive in got_src:
-        arrive()
-    got_src = forward(srcX)
-    got_hx = copy(H.at[0:2], HX, axial_id(1), c < C - 1, c > 0)
-
     def inflow(v, a, ap, am):
         x = v[a]
         r, l = wr[a], wl[a]
@@ -303,16 +338,28 @@
             each(one)
 
     def gather(final, ret):
+        k = slots(N - 1)
+
+        def part(peer, slot, owner=j):
+            return remote(final.at[peer], ret.at[pl.ds(pl.multiple_of(owner * rows, 8), rows), :],
+                          (s, peer, c), slot)
+
+        for i in range(1, N):
+            d = farthest(i)
+            peer = lax.rem(j + d, N)
+            part(peer, k + d - 1).start()
+        ret[pl.ds(pl.multiple_of(j * rows, 8), rows), :] = final[j]
         arrivals = []
         for d in range(1, N):
-            peer = lax.rem(j + d, N)
-            arrivals.append(copy(
-                final.at[peer], ret.at[pl.ds(pl.multiple_of(j * rows, 8), rows), :], azim_id(d)))
-        ret[pl.ds(pl.multiple_of(j * rows, 8), rows), :] = final[j]
+            pending.append((part(lax.rem(j + d, N), k + d - 1), None))
+            owner = lax.rem(j - d + N, N)
+            arrivals.append(lambda d=d, owner=owner: part(j, k + d - 1, owner).wait_recv())
         return arrivals
 
     sweeps(vA, SWEEPS - 1, finA)
     got_adj = gather(finA, retA)
+    pl.when(j == N - 1)(lambda: ring.start())
+    pending.append((ring, None))
 
     for arrive in got_prior:
         arrive()
@@ -330,7 +377,7 @@
     got_temp = gather(finT, temp)
 
     loads[3].wait()
-    got_hn()
+    ring.wait_recv()
     got_hx()
     got_hr()
 
@@ -357,10 +404,9 @@
     for arrive in got_temp:
         arrive()
     for desc, sending in pending:
-        if sending is None:
-            desc.wait_send()
-        else:
-            pl.when(sending)(lambda: desc.wait_send())
+        when(sending, lambda: desc.wait_send())
+    for final in finals:
+        final()
 
 
 def store(*refs):
@@ -384,7 +430,7 @@
     hbm = pl.BlockSpec(memory_space=pl.ANY)
     smem = pl.BlockSpec(memory_space=pltpu.SMEM)
     V = lambda *shape, dtype=f32: pltpu.VMEM(shape, dtype)
-    copies = 38 + 4 * (N - 1)
+    copies = 38 + 8 * (N - 1)
     wide = (N, ext, 2 * L)
     misfit, dual, temp = pl.pallas_call(
         functools.partial(kernel, sizes),

time: 42 us -> 38.9 us (0.926)
  the two profiles are of different devices: /device:TPU:30 before, /device:TPU:1 now
where the time goes in v1:
time: 38.9 us; the launch traced here: 38.8 us
  Pallas kernels  38.1 us (98%)
  between operations  0.64 us (2%)
    pallas_call x1, Pallas kernels, body(): pl.pallas_call(functools.partial(kernel, sizes), out_shape=(V(3, R, L), V...  37.2 us
    pallas_call x1, Pallas kernels, body(): pl.pallas_call(store, out_shape=tuple((jax.ShapeDtypeStruct(x.shape, f32)...  0.94 us

profile of v1, /device:TPU:1, one launch (start us, length us, event | category | flops | bytes accessed | tf_op | source)
XLA Modules:
  0.0 38.8 jit_solution(11566270833949467118)
XLA Ops:
  0.6 37.2 %shard_map.148 = (f32[3,256,128]{2,1,0:T(8,128)S(1)}, f32[3,256,128]{2,1,0:T(8,128)S(1)}, f32[256,128]{1,0:T(8,128)S(1)}) custom-call(f32[3,256,128]{2,1,0:T(8,128)} %bitcast.11, f32[3,256,128]{2,1,0:T(8,128)} %bitcast.12, s32[256,128]{1,0:T(8,128)} %bitcast.13, s32[4,128]{1,0:T(4,128)} %refs_3_.1, s32[1,128]{1,0:T(1,128)} %bitcast.14, f32[8]{0:T(128)} %refs_5_.1, ...), custom_call_target="tpu_custom_call" | custom-call | tf_op jit(solution)/shard_map/pallas_call | solution.py:435
  37.8 0.9 %shard_map.149 = (f32[3,256,128]{2,1,0:T(8,128)}, f32[3,256,128]{2,1,0:T(8,128)}, f32[256,128]{1,0:T(8,128)}) custom-call(f32[3,256,128]{2,1,0:T(8,128)S(1)} %get-tuple-element.9.refs_0_, f32[3,256,128]{2,1,0:T(8,128)S(1)} %get-tuple-element.10.refs_1_, f32[256,128]{1,0:T(8,128)S(1)} %get-tuple-element.11.refs_2_), custom_call_target="tpu_custom_call" | custom-call | tf_op jit(solution)/shard_map/pallas_call | solution.py:452

commit v2 on v1

--- a/solution.py
+++ b/solution.py
@@ -24,10 +24,11 @@
 
 def kernel(sizes, *refs):
     S, N, C = sizes
-    (A_hbm, J_hbm, fixed, spin, offs, t_rel, t_eddy, t_loss, t_plane, t_axial, t_cap, prior, goal,
+    (A_hbm, J_hbm, fixed_hbm, spin_hbm, offs_hbm, *tables_hbm, prior, goal,
      misfit, dual, temp,
+     fixed, spin, offs, t_rel, t_eddy, t_loss, t_plane, t_axial, t_cap,
      AN, AX, AR, HN, HX, HR, regE, lossM, srcE, flux, H,
-     priorX, goalX, regX, srcX,
+     priorX, goalX, regX, srcX, priorS, goalS, regS, srcS, priorP, goalP, regP, srcP,
      wa, wr, wl, inv, capH, rhsT, vT, vA, finT, finA, retA,
      A, J, relayG, relayP, local, send, recv) = refs
     R, L = fixed.shape
@@ -55,12 +56,17 @@
 
     loads = [
         pltpu.make_async_copy(A_hbm, A, local.at[0]),
-        pltpu.make_async_copy(goal, goalX.at[1, :, pl.ds(RIM, rows), :], local.at[1]),
-        pltpu.make_async_copy(prior, priorX.at[1, :, pl.ds(RIM, rows), :], local.at[2]),
+        pltpu.make_async_copy(goal, goalX.at[:, pl.ds(RIM, rows), :], local.at[1]),
+        pltpu.make_async_copy(prior, priorX.at[:, pl.ds(RIM, rows), :], local.at[2]),
         pltpu.make_async_copy(J_hbm, J, local.at[3]),
     ]
+    tables = (t_rel, t_eddy, t_loss, t_plane, t_axial, t_cap)
+    maps = [pltpu.make_async_copy(src, dst, local.at[4 + k]) for k, (src, dst) in enumerate(
+        zip((fixed_hbm, spin_hbm, offs_hbm, *tables_hbm), (fixed, spin, offs, *tables)))]
+    loads = maps + loads
     for load in loads:
         load.start()
+    loads = loads[len(maps):]
 
     counter = [0]
     pending = []
@@ -97,25 +103,39 @@
     top, bottom = j == 0, j == N - 1
     before, after = s > 0, s < S - 1
 
-    def forward(X):
-        return [copy(X.at[1], X.at[2], axial_id(-1), c > 0, c < C - 1),
-                copy(X.at[1], X.at[0], axial_id(1), c < C - 1, c > 0)]
-
-    def centre(src, X):
-        part = pl.ds(RIM, rows)
-        return [copy(src, X.at[2, :, part, :], axial_id(-1), c > 0, c < C - 1),
-                copy(src, X.at[0, :, part, :], axial_id(1), c < C - 1, c > 0)]
-
-    def outer(X):
-        arrivals = []
-        for part in (pl.ds(0, RIM), pl.ds(RIM + rows, RIM)):
-            own = X.at[1, :, part, :]
-            arrivals.append(copy(own, X.at[2, :, part, :], axial_id(-1), c > 0, c < C - 1))
-            arrivals.append(copy(own, X.at[0, :, part, :], axial_id(1), c < C - 1, c > 0))
-        return arrivals
+    up = lambda x, axis: pltpu.roll(x, x.shape[axis] - 1, axis)
+    down = lambda x, axis: pltpu.roll(x, 1, axis)
+
+    def each(f):
+        if N <= 8:
+            for a in range(N):
+                f(a, (a + 1) % N, (a + N - 1) % N)
+        else:
+            def step(a, carry):
+                f(a, lax.rem(a + 1, N), lax.rem(a + N - 1, N))
+                return carry
+            lax.fori_loop(0, N, step, 0)
+
+    G = L // N
+    assert G >= SWEEPS
+    place = lax.broadcasted_iota(jnp.int32, (ext, L), 1) // G
+
+    def forward(X, sides, packed):
+        def add(a, ap, am):
+            x = pltpu.roll(X[a], a * G, 1)
+            first = isinstance(a, int) and a == 0
+            packed[0] = x if first else jnp.where(place == a, x, packed[0])
+            packed[1] = x if first else jnp.where(place == am, x, packed[1])
+        each(add)
+        return [copy(packed.at[0], sides.at[1], axial_id(-1), c > 0, c < C - 1),
+                copy(packed.at[1], sides.at[0], axial_id(1), c < C - 1, c > 0)]
+
+    def wide(X, sides, a):
+        beside = jnp.where(place == a, sides[1], sides[0])
+        return jnp.concatenate([X[a], pltpu.roll(beside, (L - a * G) % L, 1)], axis=1)
 
     def rims(src, X, relay):
-        low, high = X.at[1, :, pl.ds(0, RIM), :], X.at[1, :, pl.ds(RIM + rows, RIM), :]
+        low, high = X.at[:, pl.ds(0, RIM), :], X.at[:, pl.ds(RIM + rows, RIM), :]
         first, last = src.at[:, 0:RIM, :], src.at[:, rows - RIM:rows, :]
         arrivals = [
             copy(last, low, azim_id(1), jnp.logical_not(bottom), jnp.logical_not(top)),
@@ -139,7 +159,7 @@
             first, count = (RIM if low else 0), (inner if low or high else ext)
             return remote(
                 E.at[pl.ds(pl.multiple_of(peer * rows + first, 8), count), :],
-                target.at[1, owner, pl.ds(first, count), :], (s, peer, c), slot)
+                target.at[owner, pl.ds(first, count), :], (s, peer, c), slot)
 
         def cases(peer, f):
             pl.when(peer == 0)(lambda: f(True, False))
@@ -167,15 +187,15 @@
                 d = lax.rem(peer - j + N, N)
                 own = E.at[start if peer == 0 else R + RIM:(start if peer == 0 else R + RIM) + RIM, :]
                 away = both(there, j != peer)
-                desc = remote(own, target.at[1, j, pl.ds(start, RIM), :], (s, peer, c),
+                desc = remote(own, target.at[j, pl.ds(start, RIM), :], (s, peer, c),
                               b + jnp.where(d > 0, d - 1, 0))
                 pl.when(away)(lambda desc=desc: desc.start())
                 pending.append((desc, away))
                 for d in range(1, N):
-                    got = remote(own, target.at[1, lax.rem(j - d + N, N), pl.ds(start, RIM), :],
+                    got = remote(own, target.at[lax.rem(j - d + N, N), pl.ds(start, RIM), :],
                                  (s, peer, c), b + d - 1)
                     ends.append((got, both(there, j == peer)))
-            target[1, j] = E[pl.ds(pl.multiple_of(j * rows, 8), ext), :]
+            target[j] = E[pl.ds(pl.multiple_of(j * rows, 8), ext), :]
 
             def arrived():
                 for d in range(1, N):
@@ -191,6 +211,9 @@
     got_an = copy(A_hbm.at[1:3], AN, azim_id(-1))
     got_ax = copy(A_hbm.at[0:2], AX, axial_id(-1), c > 0, c < C - 1)
     got_ar = copy(A_hbm.at[:, 0:RIM, :], AR, section_id(-1), before, after)
+
+    for load in maps:
+        load.wait()
 
     lane = lax.broadcasted_iota(jnp.int32, (R, L), 1)
     row = lax.broadcasted_iota(jnp.int32, (R, L), 0)
@@ -206,7 +229,6 @@
     rest_reg = spread(regE, regX)
     rest_goal = rims(goal, goalX, relayG)
     rest_prior = rims(prior, priorX, relayP)
-    goal_centre, prior_centre = centre(goal, goalX), centre(prior, priorX)
     lossM[...] = pick(bits_of(regE[RIM:RIM + R, :]), t_loss)
     got_reg = rest_reg()
     got_goal, got_prior = rest_goal(), rest_prior()
@@ -242,20 +264,22 @@
     H[2] = reluct * flux[2]
     got_hr = copy(H.at[:, R - RIM:R, :], HR, section_id(1), after, before)
     got_src = rest_src()
+    ring = [remote(H.at[1 + i // 1], HN.at[i // 1], azim_id(1), slots(1)) for i in range(2)]
+    pending.extend((piece, None) for piece in ring)
 
     got_reg()
-    got_reg = forward(regX)
+    got_reg = forward(regX, regS, regP)
     for load, arrivals in ((loads[1], got_goal), (loads[2], got_prior)):
         load.wait()
         for arrive in arrivals:
             arrive()
-    got_goal = goal_centre + outer(goalX)
-    got_prior = prior_centre + outer(priorX)
+    got_goal = forward(goalX, goalS, goalP)
+    got_prior = forward(priorX, priorS, priorP)
 
     got_src()
-    got_src = forward(srcX)
-    ring = remote(H.at[1:3], HN, azim_id(1), slots(1))
-    pl.when(j < N - 1)(lambda: ring.start())
+    got_src = forward(srcX, srcS, srcP)
+    ring[0].start()
+    pl.when(j < N - 1)(lambda: ring[1].start())
     got_hx = copy(H.at[0:2], HX, axial_id(1), c < C - 1, c > 0)
 
     def ext_mask():
@@ -267,29 +291,11 @@
         ok = jnp.logical_and(ok, jnp.logical_not(jnp.logical_and(right, c == C - 1)))
         return jnp.logical_and(ok, jnp.logical_not(jnp.logical_and(left, c == 0)))
 
-    half = lax.broadcasted_iota(jnp.int32, (ext, L), 1) < L // 2
-
-    def wide(X, a):
-        return jnp.concatenate([X[1, a], jnp.where(half, X[2, a], X[0, a])], axis=1)
-
-    up = lambda x, axis: pltpu.roll(x, x.shape[axis] - 1, axis)
-    down = lambda x, axis: pltpu.roll(x, 1, axis)
-
-    def each(f):
-        if N <= 8:
-            for a in range(N):
-                f(a, (a + 1) % N, (a + N - 1) % N)
-        else:
-            def step(a, carry):
-                f(a, lax.rem(a + 1, N), lax.rem(a + N - 1, N))
-                return carry
-            lax.fori_loop(0, N, step, 0)
-
     for arrive in got_reg:
         arrive()
 
     def first(a, ap, am):
-        bits = bits_of(wide(regX, a))
+        bits = bits_of(wide(regX, regS, a))
         ok = ext_mask()
         plane = jnp.where(ok, pick(bits, t_plane), 0.0)
         axial = jnp.where(ok, pick(bits, t_axial), 0.0)
@@ -319,7 +325,7 @@
         arrive()
 
     def adjoint_first(a, ap, am):
-        rhs = jnp.where(ext_mask(), wide(goalX, a), 0.0)
+        rhs = jnp.where(ext_mask(), wide(goalX, goalS, a), 0.0)
         rhsT[a] = rhs
         vA[0, a] = rhs * inv[a]
 
@@ -358,8 +364,7 @@
 
     sweeps(vA, SWEEPS - 1, finA)
     got_adj = gather(finA, retA)
-    pl.when(j == N - 1)(lambda: ring.start())
-    pending.append((ring, None))
+    pl.when(j == N - 1)(lambda: ring[1].start())
 
     for arrive in got_prior:
         arrive()
@@ -368,16 +373,17 @@
 
     def thermal_first(a, ap, am):
         ok = ext_mask()
-        start = jnp.where(ok, wide(priorX, a), 0.0)
+        start = jnp.where(ok, wide(priorX, priorS, a), 0.0)
         vT[0, a] = start
-        rhsT[a] = capH[a] * start + jnp.where(ok, wide(srcX, a), 0.0)
+        rhsT[a] = capH[a] * start + jnp.where(ok, wide(srcX, srcS, a), 0.0)
 
     each(thermal_first)
     sweeps(vT, SWEEPS, finT)
     got_temp = gather(finT, temp)
 
     loads[3].wait()
-    ring.wait_recv()
+    for piece in ring:
+        piece.wait_recv()
     got_hx()
     got_hr()
 
@@ -428,22 +434,24 @@
     f32 = jnp.float32
     vmem = pl.BlockSpec(memory_space=pltpu.VMEM)
     hbm = pl.BlockSpec(memory_space=pl.ANY)
-    smem = pl.BlockSpec(memory_space=pltpu.SMEM)
     V = lambda *shape, dtype=f32: pltpu.VMEM(shape, dtype)
-    copies = 38 + 8 * (N - 1)
+    copies = 48 + 8 * (N - 1)
     wide = (N, ext, 2 * L)
     misfit, dual, temp = pl.pallas_call(
         functools.partial(kernel, sizes),
         out_shape=(V(3, R, L), V(3, R, L), V(R, L)),
-        in_specs=[hbm] * 2 + [vmem] * 3 + [smem] * 6 + [hbm] * 2,
+        in_specs=[hbm] * 13,
         out_specs=(vmem, vmem, vmem),
         scratch_shapes=[
+            V(R, L, dtype=jnp.int32), V(*spin.shape, dtype=jnp.int32), V(1, L, dtype=jnp.int32),
+            *[pltpu.SMEM(table.shape, f32) for table in (rel, eddy, loss, plane, axial, cap)],
             V(2, R, L), V(2, R, L), V(3, RIM, L), V(2, R, L), V(2, R, L), V(3, RIM, L),
             V(R + 2 * RIM, L, dtype=jnp.int32), V(R, L), V(R + 2 * RIM, L), V(3, R, L), V(3, R, L),
-            V(3, N, ext, L), V(3, N, ext, L), V(3, N, ext, L, dtype=jnp.int32), V(3, N, ext, L),
+            V(N, ext, L), V(N, ext, L), V(N, ext, L, dtype=jnp.int32), V(N, ext, L),
+            *[V(2, ext, L, dtype=kind) for kind in (f32, f32, jnp.int32, f32)] * 2,
             V(*wide), V(*wide), V(*wide), V(*wide), V(*wide), V(*wide), V(2, *wide), V(2, *wide),
             V(N, rows, L), V(N, rows, L), V(R, L), V(3, R, L), V(3, R, L),
-            V(2, N, RIM, L), V(2, N, RIM, L), pltpu.SemaphoreType.DMA((4,)),
+            V(2, N, RIM, L), V(2, N, RIM, L), pltpu.SemaphoreType.DMA((13,)),
             pltpu.SemaphoreType.DMA((copies,)), pltpu.SemaphoreType.DMA((copies,)),
         ],
         compiler_params=pltpu.CompilerParams(collective_id=0, has_side_effects=True),

time: 38.9 us -> 36.6 us (0.941)
  the two profiles are of different devices: /device:TPU:1 before, /device:TPU:0 now
where the time goes in v2:
time: 36.6 us; the launch traced here: 36.5 us
  Pallas kernels  35.8 us (98%)
  between operations  0.64 us (2%)
    pallas_call x1, Pallas kernels, body(): pl.pallas_call(functools.partial(kernel, sizes), out_shape=(V(3, R, L), V...  34.9 us
    pallas_call x1, Pallas kernels, body(): pl.pallas_call(store, out_shape=tuple((jax.ShapeDtypeStruct(x.shape, f32)...  0.94 us

profile of v2, /device:TPU:0, one launch (start us, length us, event | category | flops | bytes accessed | tf_op | source)
XLA Modules:
  0.0 36.5 jit_solution(14650012852589772069)
XLA Ops:
  0.6 34.9 %shard_map.148 = (f32[3,256,128]{2,1,0:T(8,128)S(1)}, f32[3,256,128]{2,1,0:T(8,128)S(1)}, f32[256,128]{1,0:T(8,128)S(1)}) custom-call(f32[3,256,128]{2,1,0:T(8,128)} %bitcast.11, f32[3,256,128]{2,1,0:T(8,128)} %bitcast.12, s32[256,128]{1,0:T(8,128)} %bitcast.13, s32[4,128]{1,0:T(4,128)} %refs_3_.1, s32[1,128]{1,0:T(1,128)} %bitcast.14, f32[8]{0:T(128)} %refs_5_.1, ...), custom_call_target="tpu_custom_call" | custom-call | tf_op jit(solution)/shard_map/pallas_call | solution.py:440
  35.5 0.9 %shard_map.149 = (f32[3,256,128]{2,1,0:T(8,128)}, f32[3,256,128]{2,1,0:T(8,128)}, f32[256,128]{1,0:T(8,128)}) custom-call(f32[3,256,128]{2,1,0:T(8,128)S(1)} %get-tuple-element.9.refs_0_, f32[3,256,128]{2,1,0:T(8,128)S(1)} %get-tuple-element.10.refs_1_, f32[256,128]{1,0:T(8,128)S(1)} %get-tuple-element.11.refs_2_), custom_call_target="tpu_custom_call" | custom-call | tf_op jit(solution)/shard_map/pallas_call | solution.py:460

commit v3 on v2

--- a/solution.py
+++ b/solution.py
@@ -26,7 +26,7 @@
     S, N, C = sizes
     (A_hbm, J_hbm, fixed_hbm, spin_hbm, offs_hbm, *tables_hbm, prior, goal,
      misfit, dual, temp,
-     fixed, spin, offs, t_rel, t_eddy, t_loss, t_plane, t_axial, t_cap,
+     turned, fixed, spin, offs, t_rel, t_eddy, t_loss, t_plane, t_axial, t_cap,
      AN, AX, AR, HN, HX, HR, regE, lossM, srcE, flux, H,
      priorX, goalX, regX, srcX, priorS, goalS, regS, srcS, priorP, goalP, regP, srcP,
      wa, wr, wl, inv, capH, rhsT, vT, vA, finT, finA, retA,
@@ -88,6 +88,9 @@
         else:
             pl.when(cond)(f)
 
+    def unless(cond, f):
+        when(None if cond is None else jnp.logical_not(cond), f)
+
     def copy(src, dst, device, sending=None, receiving=None):
         desc = remote(src, dst, device, slots(1))
         when(sending, lambda: desc.start())
@@ -140,19 +143,20 @@
         arrivals = [
             copy(last, low, azim_id(1), jnp.logical_not(bottom), jnp.logical_not(top)),
             copy(first, high, azim_id(-1), jnp.logical_not(top), jnp.logical_not(bottom))]
-        crossed = [
-            copy(last, relay.at[0], section_id(1), both(bottom, after), both(bottom, before)),
-            copy(first, relay.at[1], section_id(-1), both(top, before), both(top, after))]
-
-        def relayed():
-            for arrive in crossed:
-                arrive()
-            arrivals.append(copy(relay.at[0], low, azim_id(1), both(bottom, before), both(top, before)))
+        down_hop = copy(last, relay.at[0], azim_id(1), both(bottom, after), both(top, after))
+        up_hop = copy(first, relay.at[1], section_id(-1), both(top, before), both(top, after))
+
+        def early():
+            up_hop()
             arrivals.append(copy(relay.at[1], high, azim_id(-1), both(top, after), both(bottom, after)))
+
+        def late():
+            down_hop()
+            arrivals.append(copy(relay.at[0], low, section_id(1), both(top, after), both(top, before)))
             return arrivals
-        return relayed
-
-    def spread(E, target):
+        return early, late
+
+    def spread(E, target, known=lambda peer: None):
         inner = ext - RIM
 
         def block(peer, slot, low, high, owner=j):
@@ -170,11 +174,12 @@
         for i in range(1, N):
             d = farthest(i)
             peer = lax.rem(j + d, N)
-            cases(peer, lambda low, high: block(peer, k + d - 1, low, high).start())
+            unless(known(peer), lambda: cases(
+                peer, lambda low, high: block(peer, k + d - 1, low, high).start()))
         for d in range(1, N):
             peer = lax.rem(j + d, N)
-            finals.append(lambda peer=peer, d=d: cases(
-                peer, lambda low, high: block(peer, k + d - 1, low, high).wait_send()))
+            finals.append(lambda peer=peer, d=d: unless(known(peer), lambda: cases(
+                peer, lambda low, high: block(peer, k + d - 1, low, high).wait_send())))
         edges = [copy(E.at[R:R + RIM, :], E.at[0:RIM, :], section_id(1), after, before),
                  copy(E.at[RIM:2 * RIM, :], E.at[R + RIM:R + 2 * RIM, :], section_id(-1), before, after)]
 
@@ -200,7 +205,8 @@
             def arrived():
                 for d in range(1, N):
                     owner = lax.rem(j - d + N, N)
-                    cases(j, lambda low, high: block(j, k + d - 1, low, high, owner).wait_recv())
+                    unless(known(j), lambda: cases(
+                        j, lambda low, high: block(j, k + d - 1, low, high, owner).wait_recv()))
                 for got, here in ends:
                     pl.when(here)(lambda got=got: got.wait_recv())
             return arrived
@@ -217,21 +223,31 @@
 
     lane = lax.broadcasted_iota(jnp.int32, (R, L), 1)
     row = lax.broadcasted_iota(jnp.int32, (R, L), 0)
-    shift = j - offs[...]
-    shift = jnp.broadcast_to(jnp.where(shift < 0, shift + N, shift), (RROT, L))
-    rotor = jnp.zeros((RROT, L), jnp.float32)
     for m in range(N):
         column = jnp.transpose(jnp.broadcast_to(spin[m:m + 1, :].astype(jnp.float32), (L, RROT)))
-        rotor = jnp.where(shift == m, column, rotor)
+        turned[m, RIM:RIM + RROT, :] = column.astype(jnp.int32)
+
+    def rotor(a, part, count):
+        shift = a - offs[...]
+        shift = jnp.broadcast_to(jnp.where(shift < 0, shift + N, shift), (count, L))
+        value = turned[0, part, :]
+        for m in range(1, N):
+            value = jnp.where(shift == m, turned[m, part, :], value)
+        return value
+
+    def in_rotor(peer):
+        return both(s == 0, (peer + 1) * rows + RIM <= RROT)
+
     regE[RIM:RIM + R, :] = fixed[...]
-    regE[RIM:RIM + RROT, :] = jnp.where(s == 0, rotor.astype(jnp.int32), fixed[0:RROT, :])
-
-    rest_reg = spread(regE, regX)
-    rest_goal = rims(goal, goalX, relayG)
-    rest_prior = rims(prior, priorX, relayP)
+    regE[RIM:RIM + RROT, :] = jnp.where(s == 0, rotor(j, pl.ds(RIM, RROT), RROT), fixed[0:RROT, :])
+
+    rest_reg = spread(regE, regX, in_rotor)
+    goal_early, goal_late = rims(goal, goalX, relayG)
+    prior_early, prior_late = rims(prior, priorX, relayP)
     lossM[...] = pick(bits_of(regE[RIM:RIM + R, :]), t_loss)
     got_reg = rest_reg()
-    got_goal, got_prior = rest_goal(), rest_prior()
+    goal_early()
+    prior_early()
 
     loads[0].wait()
 
@@ -266,8 +282,20 @@
     got_src = rest_src()
     ring = [remote(H.at[1 + i // 1], HN.at[i // 1], azim_id(1), slots(1)) for i in range(2)]
     pending.extend((piece, None) for piece in ring)
+    pl.when(both(j == N - 1, s == 0))(lambda: ring[0].start())
+    pl.when(both(j == N - 1, s == 0))(lambda: ring[1].start())
+
+    got_goal, got_prior = goal_late(), prior_late()
 
     got_reg()
+
+    def own_rotor():
+        def one(a, ap, am):
+            regX[a] = rotor(a, pl.ds(pl.multiple_of(j * rows, 8), ext), ext)
+        each(one)
+
+    if RIM + rows <= RROT:
+        pl.when(in_rotor(j))(own_rotor)
     got_reg = forward(regX, regS, regP)
     for load, arrivals in ((loads[1], got_goal), (loads[2], got_prior)):
         load.wait()
@@ -278,7 +306,8 @@
 
     got_src()
     got_src = forward(srcX, srcS, srcP)
-    ring[0].start()
+    pl.when(j < N - 1)(lambda: ring[0].start())
+    pl.when(both(j == N - 1, s > 0))(lambda: ring[0].start())
     pl.when(j < N - 1)(lambda: ring[1].start())
     got_hx = copy(H.at[0:2], HX, axial_id(1), c < C - 1, c > 0)
 
@@ -364,7 +393,7 @@
 
     sweeps(vA, SWEEPS - 1, finA)
     got_adj = gather(finA, retA)
-    pl.when(j == N - 1)(lambda: ring[1].start())
+    pl.when(both(j == N - 1, s > 0))(lambda: ring[1].start())
 
     for arrive in got_prior:
         arrive()
@@ -443,6 +472,7 @@
         in_specs=[hbm] * 13,
         out_specs=(vmem, vmem, vmem),
         scratch_shapes=[
+            V(spin.shape[0], max(RIM + spin.shape[1], ext), L, dtype=jnp.int32),
             V(R, L, dtype=jnp.int32), V(*spin.shape, dtype=jnp.int32), V(1, L, dtype=jnp.int32),
             *[pltpu.SMEM(table.shape, f32) for table in (rel, eddy, loss, plane, axial, cap)],
             V(2, R, L), V(2, R, L), V(3, RIM, L), V(2, R, L), V(2, R, L), V(3, RIM, L),

time: 36.6 us -> 33.9 us (0.926)
  the two profiles are of different devices: /device:TPU:0 before, /device:TPU:3 now
where the time goes in v3:
time: 33.9 us; the launch traced here: 33.8 us
  Pallas kernels  33.2 us (98%)
  between operations  0.64 us (2%)
    pallas_call x1, Pallas kernels, body(): pl.pallas_call(functools.partial(kernel, sizes), out_shape=(V(3, R, L), V...  32.2 us
    pallas_call x1, Pallas kernels, body(): pl.pallas_call(store, out_shape=tuple((jax.ShapeDtypeStruct(x.shape, f32)...  0.94 us

profile of v3, /device:TPU:3, one launch (start us, length us, event | category | flops | bytes accessed | tf_op | source)
XLA Modules:
  0.0 33.8 jit_solution(2055160888864031838)
XLA Ops:
  0.6 32.2 %shard_map.148 = (f32[3,256,128]{2,1,0:T(8,128)S(1)}, f32[3,256,128]{2,1,0:T(8,128)S(1)}, f32[256,128]{1,0:T(8,128)S(1)}) custom-call(f32[3,256,128]{2,1,0:T(8,128)} %bitcast.11, f32[3,256,128]{2,1,0:T(8,128)} %bitcast.12, s32[256,128]{1,0:T(8,128)} %bitcast.13, s32[4,128]{1,0:T(4,128)} %refs_3_.1, s32[1,128]{1,0:T(1,128)} %bitcast.14, f32[8]{0:T(128)} %refs_5_.1, ...), custom_call_target="tpu_custom_call" | custom-call | tf_op jit(solution)/shard_map/pallas_call | solution.py:469
  32.9 0.9 %shard_map.149 = (f32[3,256,128]{2,1,0:T(8,128)}, f32[3,256,128]{2,1,0:T(8,128)}, f32[256,128]{1,0:T(8,128)}) custom-call(f32[3,256,128]{2,1,0:T(8,128)S(1)} %get-tuple-element.9.refs_0_, f32[3,256,128]{2,1,0:T(8,128)S(1)} %get-tuple-element.10.refs_1_, f32[256,128]{1,0:T(8,128)S(1)} %get-tuple-element.11.refs_2_), custom_call_target="tpu_custom_call" | custom-call | tf_op jit(solution)/shard_map/pallas_call | solution.py:490

commit v4 on v3

--- a/solution.py
+++ b/solution.py
@@ -30,7 +30,7 @@
      AN, AX, AR, HN, HX, HR, regE, lossM, srcE, flux, H,
      priorX, goalX, regX, srcX, priorS, goalS, regS, srcS, priorP, goalP, regP, srcP,
      wa, wr, wl, inv, capH, rhsT, vT, vA, finT, finA, retA,
-     A, J, relayG, relayP, local, send, recv) = refs
+     A, J, edge, beside, relay, local, send, recv) = refs
     R, L = fixed.shape
     rows = prior.shape[1]
     RROT = spin.shape[1]
@@ -68,18 +68,19 @@
         load.start()
     loads = loads[len(maps):]
 
-    counter = [0]
+    used = [0, 0]
     pending = []
     finals = []
 
-    def slots(count):
-        k = counter[0]
-        counter[0] += count
-        return k
-
-    def remote(src, dst, device, k):
+    def slots(sends=1, receives=1):
+        first = tuple(used)
+        used[0] += sends
+        used[1] += receives
+        return first
+
+    def remote(src, dst, device, slot, d=0):
         return pltpu.make_async_remote_copy(
-            src_ref=src, dst_ref=dst, send_sem=send.at[k], recv_sem=recv.at[k],
+            src_ref=src, dst_ref=dst, send_sem=send.at[slot[0] + d], recv_sem=recv.at[slot[1] + d],
             device_id=device, device_id_type=MESH)
 
     def when(cond, f):
@@ -91,8 +92,8 @@
     def unless(cond, f):
         when(None if cond is None else jnp.logical_not(cond), f)
 
-    def copy(src, dst, device, sending=None, receiving=None):
-        desc = remote(src, dst, device, slots(1))
+    def copy(src, dst, device, sending=None, receiving=None, slot=None):
+        desc = remote(src, dst, device, slot or slots())
         when(sending, lambda: desc.start())
         pending.append((desc, sending))
         return lambda: when(receiving, lambda: desc.wait_recv())
@@ -137,49 +138,75 @@
         beside = jnp.where(place == a, sides[1], sides[0])
         return jnp.concatenate([X[a], pltpu.roll(beside, (L - a * G) % L, 1)], axis=1)
 
-    def rims(src, X, relay):
-        low, high = X.at[:, pl.ds(0, RIM), :], X.at[:, pl.ds(RIM + rows, RIM), :]
-        first, last = src.at[:, 0:RIM, :], src.at[:, rows - RIM:rows, :]
+    half = RIM // 2
+    assert half >= SWEEPS
+
+    def rims(edge, beside, relay):
+        upper = lax.broadcasted_iota(jnp.int32, (RIM, L), 0) < half
+
+        def cut(a, ap, am):
+            def tile(X, first):
+                return X[a, first:first + RIM, :]
+            edge[0, a] = jnp.where(upper, pltpu.roll(tile(priorX, rows), half, 0), tile(goalX, rows))
+            edge[1, a] = jnp.where(upper, tile(goalX, RIM), pltpu.roll(tile(priorX, RIM), half, 0))
+        each(cut)
+        low, high, last, first = beside.at[0], beside.at[1], edge.at[0], edge.at[1]
+        (to_next, at_low), (to_last, at_high), (turn_low, at_first), (turn_high, at_second) = (
+            slots() for _ in range(4))
         arrivals = [
-            copy(last, low, azim_id(1), jnp.logical_not(bottom), jnp.logical_not(top)),
-            copy(first, high, azim_id(-1), jnp.logical_not(top), jnp.logical_not(bottom))]
-        down_hop = copy(last, relay.at[0], azim_id(1), both(bottom, after), both(top, after))
-        up_hop = copy(first, relay.at[1], section_id(-1), both(top, before), both(top, after))
+            copy(last, low, azim_id(1), jnp.logical_not(bottom), jnp.logical_not(top), (to_next, at_low)),
+            copy(first, high, azim_id(-1), jnp.logical_not(top), jnp.logical_not(bottom), (to_last, at_high))]
+        down_hop = copy(last, relay.at[0], azim_id(1), both(bottom, after), both(top, after),
+                        (to_next, at_first))
+        up_hop = copy(first, relay.at[1], section_id(-1), both(top, before), both(top, after),
+                      (to_last, at_second))
 
         def early():
             up_hop()
-            arrivals.append(copy(relay.at[1], high, azim_id(-1), both(top, after), both(bottom, after)))
+            arrivals.append(copy(relay.at[1], high, azim_id(-1), both(top, after), both(bottom, after),
+                                 (turn_high, at_high)))
 
         def late():
             down_hop()
-            arrivals.append(copy(relay.at[0], low, section_id(1), both(top, after), both(top, before)))
-            return arrivals
+            arrivals.append(copy(relay.at[0], low, section_id(1), both(top, after), both(top, before),
+                                 (turn_low, at_low)))
+
+            def arrived():
+                for arrive in arrivals:
+                    arrive()
+
+                def spread_rims(a, ap, am):
+                    for k, first in ((0, 0), (1, RIM + rows)):
+                        goalX[a, first:first + RIM, :] = beside[k, a]
+                        priorX[a, first:first + RIM, :] = pltpu.roll(beside[k, a], half, 0)
+                each(spread_rims)
+            return arrived
         return early, late
 
     def spread(E, target, known=lambda peer: None):
         inner = ext - RIM
 
-        def block(peer, slot, low, high, owner=j):
+        def block(peer, d, low, high, owner=j):
             first, count = (RIM if low else 0), (inner if low or high else ext)
             return remote(
                 E.at[pl.ds(pl.multiple_of(peer * rows + first, 8), count), :],
-                target.at[owner, pl.ds(first, count), :], (s, peer, c), slot)
+                target.at[owner, pl.ds(first, count), :], (s, peer, c), k, d - 1)
 
         def cases(peer, f):
             pl.when(peer == 0)(lambda: f(True, False))
             pl.when(peer == N - 1)(lambda: f(False, True))
             pl.when(both(peer > 0, peer < N - 1))(lambda: f(False, False))
 
-        k = slots(N - 1)
+        k = slots(N - 1, N - 1)
         for i in range(1, N):
             d = farthest(i)
             peer = lax.rem(j + d, N)
             unless(known(peer), lambda: cases(
-                peer, lambda low, high: block(peer, k + d - 1, low, high).start()))
+                peer, lambda low, high: block(peer, d, low, high).start()))
         for d in range(1, N):
             peer = lax.rem(j + d, N)
             finals.append(lambda peer=peer, d=d: unless(known(peer), lambda: cases(
-                peer, lambda low, high: block(peer, k + d - 1, low, high).wait_send())))
+                peer, lambda low, high: block(peer, d, low, high).wait_send())))
         edges = [copy(E.at[R:R + RIM, :], E.at[0:RIM, :], section_id(1), after, before),
                  copy(E.at[RIM:2 * RIM, :], E.at[R + RIM:R + 2 * RIM, :], section_id(-1), before, after)]
 
@@ -187,18 +214,19 @@
             for arrive in edges:
                 arrive()
             ends = []
+            _, come = slots(0, N - 1)
             for peer, start, there in ((0, 0, before), (N - 1, RIM + rows, after)):
-                b = slots(N - 1)
+                go, _ = slots(1, 0)
                 d = lax.rem(peer - j + N, N)
                 own = E.at[start if peer == 0 else R + RIM:(start if peer == 0 else R + RIM) + RIM, :]
                 away = both(there, j != peer)
                 desc = remote(own, target.at[j, pl.ds(start, RIM), :], (s, peer, c),
-                              b + jnp.where(d > 0, d - 1, 0))
+                              (go, come + jnp.where(d > 0, d - 1, 0)))
                 pl.when(away)(lambda desc=desc: desc.start())
                 pending.append((desc, away))
                 for d in range(1, N):
                     got = remote(own, target.at[lax.rem(j - d + N, N), pl.ds(start, RIM), :],
-                                 (s, peer, c), b + d - 1)
+                                 (s, peer, c), (go, come + d - 1))
                     ends.append((got, both(there, j == peer)))
             target[j] = E[pl.ds(pl.multiple_of(j * rows, 8), ext), :]
 
@@ -206,7 +234,7 @@
                 for d in range(1, N):
                     owner = lax.rem(j - d + N, N)
                     unless(known(j), lambda: cases(
-                        j, lambda low, high: block(j, k + d - 1, low, high, owner).wait_recv()))
+                        j, lambda low, high: block(j, d, low, high, owner).wait_recv()))
                 for got, here in ends:
                     pl.when(here)(lambda got=got: got.wait_recv())
             return arrived
@@ -242,12 +270,12 @@
     regE[RIM:RIM + RROT, :] = jnp.where(s == 0, rotor(j, pl.ds(RIM, RROT), RROT), fixed[0:RROT, :])
 
     rest_reg = spread(regE, regX, in_rotor)
-    goal_early, goal_late = rims(goal, goalX, relayG)
-    prior_early, prior_late = rims(prior, priorX, relayP)
+    loads[1].wait()
+    loads[2].wait()
+    rims_early, rims_late = rims(edge, beside, relay)
     lossM[...] = pick(bits_of(regE[RIM:RIM + R, :]), t_loss)
     got_reg = rest_reg()
-    goal_early()
-    prior_early()
+    rims_early()
 
     loads[0].wait()
 
@@ -280,12 +308,12 @@
     H[2] = reluct * flux[2]
     got_hr = copy(H.at[:, R - RIM:R, :], HR, section_id(1), after, before)
     got_src = rest_src()
-    ring = [remote(H.at[1 + i // 1], HN.at[i // 1], azim_id(1), slots(1)) for i in range(2)]
+    ring = [remote(H.at[1 + i // 1], HN.at[i // 1], azim_id(1), slots()) for i in range(2)]
     pending.extend((piece, None) for piece in ring)
     pl.when(both(j == N - 1, s == 0))(lambda: ring[0].start())
     pl.when(both(j == N - 1, s == 0))(lambda: ring[1].start())
 
-    got_goal, got_prior = goal_late(), prior_late()
+    got_rims = rims_late()
 
     got_reg()
 
@@ -297,10 +325,7 @@
     if RIM + rows <= RROT:
         pl.when(in_rotor(j))(own_rotor)
     got_reg = forward(regX, regS, regP)
-    for load, arrivals in ((loads[1], got_goal), (loads[2], got_prior)):
-        load.wait()
-        for arrive in arrivals:
-            arrive()
+    got_rims()
     got_goal = forward(goalX, goalS, goalP)
     got_prior = forward(priorX, priorS, priorP)
 
@@ -373,22 +398,22 @@
             each(one)
 
     def gather(final, ret):
-        k = slots(N - 1)
-
-        def part(peer, slot, owner=j):
+        k = slots(N - 1, N - 1)
+
+        def part(peer, d, owner=j):
             return remote(final.at[peer], ret.at[pl.ds(pl.multiple_of(owner * rows, 8), rows), :],
-                          (s, peer, c), slot)
+                          (s, peer, c), k, d - 1)
 
         for i in range(1, N):
             d = farthest(i)
             peer = lax.rem(j + d, N)
-            part(peer, k + d - 1).start()
+            part(peer, d).start()
         ret[pl.ds(pl.multiple_of(j * rows, 8), rows), :] = final[j]
         arrivals = []
         for d in range(1, N):
-            pending.append((part(lax.rem(j + d, N), k + d - 1), None))
+            pending.append((part(lax.rem(j + d, N), d), None))
             owner = lax.rem(j - d + N, N)
-            arrivals.append(lambda d=d, owner=owner: part(j, k + d - 1, owner).wait_recv())
+            arrivals.append(lambda d=d, owner=owner: part(j, d, owner).wait_recv())
         return arrivals
 
     sweeps(vA, SWEEPS - 1, finA)
@@ -442,6 +467,7 @@
         when(sending, lambda: desc.wait_send())
     for final in finals:
         final()
+    assert used == [send.shape[0], recv.shape[0]]
 
 
 def store(*refs):
@@ -464,7 +490,6 @@
     vmem = pl.BlockSpec(memory_space=pltpu.VMEM)
     hbm = pl.BlockSpec(memory_space=pl.ANY)
     V = lambda *shape, dtype=f32: pltpu.VMEM(shape, dtype)
-    copies = 48 + 8 * (N - 1)
     wide = (N, ext, 2 * L)
     misfit, dual, temp = pl.pallas_call(
         functools.partial(kernel, sizes),
@@ -481,8 +506,8 @@
             *[V(2, ext, L, dtype=kind) for kind in (f32, f32, jnp.int32, f32)] * 2,
             V(*wide), V(*wide), V(*wide), V(*wide), V(*wide), V(*wide), V(2, *wide), V(2, *wide),
             V(N, rows, L), V(N, rows, L), V(R, L), V(3, R, L), V(3, R, L),
-            V(2, N, RIM, L), V(2, N, RIM, L), pltpu.SemaphoreType.DMA((13,)),
-            pltpu.SemaphoreType.DMA((copies,)), pltpu.SemaphoreType.DMA((copies,)),
+            V(2, N, RIM, L), V(2, N, RIM, L), V(2, N, RIM, L), pltpu.SemaphoreType.DMA((13,)),
+            pltpu.SemaphoreType.DMA((27 + 4 * (N - 1),)), pltpu.SemaphoreType.DMA((23 + 6 * (N - 1),)),
         ],
         compiler_params=pltpu.CompilerParams(collective_id=0, has_side_effects=True),
     )(A.reshape(3, R, L), J.reshape(3, R, L), fixed.reshape(R, L), spin, offs.reshape(1, L),

time: 33.9 us -> 33 us (0.973)
  Pallas kernels: 33.2 us -> 32.3 us
    pallas_call x1, Pallas kernels: 32.2 us -> 31.3 us  [body(): pl.pallas_call(functools.partial(kernel, sizes), out_shape=(V(3, R, L), V...]
where the time goes in v4:
time: 33 us; the launch traced here: 32.9 us
  Pallas kernels  32.3 us (98%)
  between operations  0.64 us (2%)
    pallas_call x1, Pallas kernels, body(): pl.pallas_call(functools.partial(kernel, sizes), out_shape=(V(3, R, L), V...  31.3 us
    pallas_call x1, Pallas kernels, body(): pl.pallas_call(store, out_shape=tuple((jax.ShapeDtypeStruct(x.shape, f32)...  0.94 us

profile of v4, /device:TPU:3, one launch (start us, length us, event | category | flops | bytes accessed | tf_op | source)
XLA Modules:
  0.0 32.9 jit_solution(17272590964839720038)
XLA Ops:
  0.6 31.3 %shard_map.148 = (f32[3,256,128]{2,1,0:T(8,128)S(1)}, f32[3,256,128]{2,1,0:T(8,128)S(1)}, f32[256,128]{1,0:T(8,128)S(1)}) custom-call(f32[3,256,128]{2,1,0:T(8,128)} %bitcast.11, f32[3,256,128]{2,1,0:T(8,128)} %bitcast.12, s32[256,128]{1,0:T(8,128)} %bitcast.13, s32[4,128]{1,0:T(4,128)} %refs_3_.1, s32[1,128]{1,0:T(1,128)} %bitcast.14, f32[8]{0:T(128)} %refs_5_.1, ...), custom_call_target="tpu_custom_call" | custom-call | tf_op jit(solution)/shard_map/pallas_call | solution.py:494
  32.0 0.9 %shard_map.149 = (f32[3,256,128]{2,1,0:T(8,128)}, f32[3,256,128]{2,1,0:T(8,128)}, f32[256,128]{1,0:T(8,128)}) custom-call(f32[3,256,128]{2,1,0:T(8,128)S(1)} %get-tuple-element.9.refs_0_, f32[3,256,128]{2,1,0:T(8,128)S(1)} %get-tuple-element.10.refs_1_, f32[256,128]{1,0:T(8,128)S(1)} %get-tuple-element.11.refs_2_), custom_call_target="tpu_custom_call" | custom-call | tf_op jit(solution)/shard_map/pallas_call | solution.py:515

commit v5 on v4

--- a/solution.py
+++ b/solution.py
@@ -326,13 +326,15 @@
         pl.when(in_rotor(j))(own_rotor)
     got_reg = forward(regX, regS, regP)
     got_rims()
+    pl.when(both(j == N - 1, s > 0, c % 2 == 0))(lambda: ring[0].start())
+    pl.when(both(j < N - 1, c % 2 == 0))(lambda: ring[0].start())
     got_goal = forward(goalX, goalS, goalP)
     got_prior = forward(priorX, priorS, priorP)
 
     got_src()
     got_src = forward(srcX, srcS, srcP)
-    pl.when(j < N - 1)(lambda: ring[0].start())
-    pl.when(both(j == N - 1, s > 0))(lambda: ring[0].start())
+    pl.when(both(j == N - 1, s > 0, c % 2 == 1))(lambda: ring[0].start())
+    pl.when(both(j < N - 1, c % 2 == 1))(lambda: ring[0].start())
     pl.when(j < N - 1)(lambda: ring[1].start())
     got_hx = copy(H.at[0:2], HX, axial_id(1), c < C - 1, c > 0)
 

time: 33 us -> 32.6 us (0.988)
  Pallas kernels: 32.3 us -> 31.8 us
    pallas_call x1, Pallas kernels: 31.3 us -> 30.9 us  [body(): pl.pallas_call(functools.partial(kernel, sizes), out_shape=(V(3, R, L), V...]
where the time goes in v5:
time: 32.6 us; the launch traced here: 32.5 us
  Pallas kernels  31.8 us (98%)
  between operations  0.64 us (2%)
    pallas_call x1, Pallas kernels, body(): pl.pallas_call(functools.partial(kernel, sizes), out_shape=(V(3, R, L), V...  30.9 us
    pallas_call x1, Pallas kernels, body(): pl.pallas_call(store, out_shape=tuple((jax.ShapeDtypeStruct(x.shape, f32)...  0.94 us

profile of v5, /device:TPU:3, one launch (start us, length us, event | category | flops | bytes accessed | tf_op | source)
XLA Modules:
  0.0 32.5 jit_solution(16226370545048974982)
XLA Ops:
  0.6 30.9 %shard_map.148 = (f32[3,256,128]{2,1,0:T(8,128)S(1)}, f32[3,256,128]{2,1,0:T(8,128)S(1)}, f32[256,128]{1,0:T(8,128)S(1)}) custom-call(f32[3,256,128]{2,1,0:T(8,128)} %bitcast.11, f32[3,256,128]{2,1,0:T(8,128)} %bitcast.12, s32[256,128]{1,0:T(8,128)} %bitcast.13, s32[4,128]{1,0:T(4,128)} %refs_3_.1, s32[1,128]{1,0:T(1,128)} %bitcast.14, f32[8]{0:T(128)} %refs_5_.1, ...), custom_call_target="tpu_custom_call" | custom-call | tf_op jit(solution)/shard_map/pallas_call | solution.py:496
  31.5 0.9 %shard_map.149 = (f32[3,256,128]{2,1,0:T(8,128)}, f32[3,256,128]{2,1,0:T(8,128)}, f32[256,128]{1,0:T(8,128)}) custom-call(f32[3,256,128]{2,1,0:T(8,128)S(1)} %get-tuple-element.9.refs_0_, f32[3,256,128]{2,1,0:T(8,128)S(1)} %get-tuple-element.10.refs_1_, f32[256,128]{1,0:T(8,128)S(1)} %get-tuple-element.11.refs_2_), custom_call_target="tpu_custom_call" | custom-call | tf_op jit(solution)/shard_map/pallas_call | solution.py:517

commit v6 on v5

--- a/solution.py
+++ b/solution.py
@@ -328,6 +328,7 @@
     got_rims()
     pl.when(both(j == N - 1, s > 0, c % 2 == 0))(lambda: ring[0].start())
     pl.when(both(j < N - 1, c % 2 == 0))(lambda: ring[0].start())
+    pl.when(both(j < N - 1, c % 2 == 0))(lambda: ring[1].start())
     got_goal = forward(goalX, goalS, goalP)
     got_prior = forward(priorX, priorS, priorP)
 
@@ -335,7 +336,7 @@
     got_src = forward(srcX, srcS, srcP)
     pl.when(both(j == N - 1, s > 0, c % 2 == 1))(lambda: ring[0].start())
     pl.when(both(j < N - 1, c % 2 == 1))(lambda: ring[0].start())
-    pl.when(j < N - 1)(lambda: ring[1].start())
+    pl.when(both(j < N - 1, c % 2 == 1))(lambda: ring[1].start())
     got_hx = copy(H.at[0:2], HX, axial_id(1), c < C - 1, c > 0)
 
     def ext_mask():

time: 32.6 us -> 32.6 us (level)
  no operation moved by 1% of the time
where the time goes in v6:
time: 32.6 us; the launch traced here: 32.5 us
  Pallas kernels  31.8 us (98%)
  between operations  0.64 us (2%)
    pallas_call x1, Pallas kernels, body(): pl.pallas_call(functools.partial(kernel, sizes), out_shape=(V(3, R, L), V...  30.9 us
    pallas_call x1, Pallas kernels, body(): pl.pallas_call(store, out_shape=tuple((jax.ShapeDtypeStruct(x.shape, f32)...  0.94 us

profile of v6, /device:TPU:3, one launch (start us, length us, event | category | flops | bytes accessed | tf_op | source)
XLA Modules:
  0.0 32.5 jit_solution(1896428705446759149)
XLA Ops:
  0.6 30.9 %shard_map.148 = (f32[3,256,128]{2,1,0:T(8,128)S(1)}, f32[3,256,128]{2,1,0:T(8,128)S(1)}, f32[256,128]{1,0:T(8,128)S(1)}) custom-call(f32[3,256,128]{2,1,0:T(8,128)} %bitcast.11, f32[3,256,128]{2,1,0:T(8,128)} %bitcast.12, s32[256,128]{1,0:T(8,128)} %bitcast.13, s32[4,128]{1,0:T(4,128)} %refs_3_.1, s32[1,128]{1,0:T(1,128)} %bitcast.14, f32[8]{0:T(128)} %refs_5_.1, ...), custom_call_target="tpu_custom_call" | custom-call | tf_op jit(solution)/shard_map/pallas_call | solution.py:497
  31.5 0.9 %shard_map.149 = (f32[3,256,128]{2,1,0:T(8,128)}, f32[3,256,128]{2,1,0:T(8,128)}, f32[256,128]{1,0:T(8,128)}) custom-call(f32[3,256,128]{2,1,0:T(8,128)S(1)} %get-tuple-element.9.refs_0_, f32[3,256,128]{2,1,0:T(8,128)S(1)} %get-tuple-element.10.refs_1_, f32[256,128]{1,0:T(8,128)S(1)} %get-tuple-element.11.refs_2_), custom_call_target="tpu_custom_call" | custom-call | tf_op jit(solution)/shard_map/pallas_call | solution.py:518
